TPU v7x, 128 devices: a whole 4x4x4 slice. The times are simulated.
128 devices in a mesh: dp: 128 (over x, z, y, core).
Axes of the slice: x: 4, y: 4, z: 4, core: 2. Of those that a mesh axis runs over, the one named last changes fastest.
Arguments:
- step_index: int32 [1], replicated, may hold values from 0 to 63
- dest: int32 [2, 32768, 1], P(None, 'dp'), may hold values from 0 to 127; in each aligned block of 256 rows (0 to 255, 256 to 511, ..., all dimensions but the last counted through in order) at most 4 rows name the same one
- tokens: bfloat16 [2, 32768, 1024], P(None, 'dp'), may hold values from -6 to 6
- params: float32 [131072, 1024], P('dp'), may hold values from -0.1875 to 0.1875
- trackers: float32 [131072, 1024], P('dp'), may hold values from -4 to 4
- old_grads: float32 [131072, 1024], P('dp'), may hold values from -4 to 4
- key_weight: bfloat16 [1024, 1024], replicated, may hold values from -0.1875 to 0.1875
- latents: bfloat16 [128, 1024], replicated, may hold values from -6 to 6
- targets: float32 [16384, 1024], P('dp'), may hold values from -6 to 6
Outputs:
- new_params: float32 [131072, 1024], P('dp')
- new_trackers: float32 [131072, 1024], P('dp')
Inputs may be any that keep to these rules, and one draw needn't show every extreme that they name: `dest`: in each step no trainer receives more than 4 rows from the rows of one device, and that bound is reached; every trainer receives some row.
All inputs are finite; a program needn't handle non-finite values.
Results may differ from a plain program's by a relative error of at most 0.012.
Values may be sent and summed in bfloat16 or wider, within the bound.
A program may use at most 128 MiB of HBM per device.

v0:
```python
from functools import partial

import jax
import jax.numpy as jnp
from jax import lax
from jax.sharding import PartitionSpec as P

HEADS = 16
STEPS = 2


def from_partner(value, axis, stride):
    mask = 2**stride
    pairs = [(source, source ^ mask) for source in range(lax.axis_size(axis))]
    return lax.ppermute(value, axis, pairs)


def local_grad(weight, rows, live, key_weight, latents, target):
    win, width = rows.shape
    count_lat = latents.shape[0]
    heads = HEADS
    head_size = width // heads
    keys = jnp.dot(rows, key_weight, preferred_element_type=jnp.float32).astype(jnp.bfloat16)
    values = jnp.dot(rows, weight.astype(jnp.bfloat16), preferred_element_type=jnp.float32).astype(
        jnp.bfloat16
    )
    queries = latents.reshape(count_lat, heads, head_size)
    keyed = keys.reshape(win, heads, head_size)
    scores = jnp.einsum(
        "lhd,jhd->hlj", queries, keyed, preferred_element_type=jnp.float32
    ) / jnp.sqrt(jnp.float32(head_size))
    attn = (jax.nn.sigmoid(scores - 3.5) * live[None, None, :]).astype(jnp.bfloat16)
    out = jnp.einsum(
        "hlj,jhd->lhd",
        attn,
        values.reshape(win, heads, head_size),
        preferred_element_type=jnp.float32,
    )
    resid = ((out.reshape(count_lat, width) - target) / 16.0).astype(jnp.bfloat16)
    dvalues = jnp.einsum(
        "hlj,lhd->jhd",
        attn,
        resid.reshape(count_lat, heads, head_size),
        preferred_element_type=jnp.float32,
    )
    dvalues = dvalues.reshape(win, width).astype(jnp.bfloat16)
    return lax.dot_general(
        rows, dvalues, (((0,), (0,)), ((), ())), preferred_element_type=jnp.float32
    )


def pack_rows(owner, token_rows, count_dev):
    rows, width = token_rows.shape
    cap = 2 * rows // count_dev
    onehot = (owner[:, None] == jnp.arange(count_dev, dtype=jnp.int32)[None, :]).astype(jnp.float32)
    rank = jnp.sum(jnp.cumsum(onehot, axis=0) * onehot, axis=1).astype(jnp.int32) - 1
    where = owner * cap + rank
    buffer = jnp.zeros((count_dev * cap, width), jnp.bfloat16).at[where].set(token_rows)
    flags = (
        jnp.zeros((count_dev * cap,), jnp.bfloat16).at[where].set(jnp.ones((rows,), jnp.bfloat16))
    )
    return (buffer.reshape(count_dev, cap, width), flags.reshape(count_dev, cap))


def swap_pair(pair, bit):
    return from_partner(pair, "dp", bit)


def shards(step_index, dest, tokens, params, trackers, old_grads, key_weight, latents, targets):
    count_dev = lax.axis_size("dp")
    logn = count_dev.bit_length() - 1
    width = tokens.shape[2]
    weight = params
    tracker = trackers
    gradient = old_grads
    for step in range(STEPS):
        bit_now = (step_index[0] + step) % logn
        send_rows, send_flags = pack_rows(dest[step, :, 0], tokens[step], count_dev)
        got_rows, got_flags = (
            lax.all_to_all(send_rows, "dp", split_axis=0, concat_axis=0, tiled=True),
            lax.all_to_all(send_flags, "dp", split_axis=0, concat_axis=0, tiled=True),
        )
        rows = got_rows.reshape(-1, width)
        live = got_flags.reshape(-1).astype(jnp.float32)
        other_weight, other_track = lax.switch(
            bit_now, [partial(swap_pair, bit=item) for item in range(logn)], (weight, tracker)
        )
        new_weight = 0.5 * (weight + other_weight) - 0.05 * tracker
        new_grad = local_grad(new_weight, rows, live, key_weight, latents, targets)
        tracker = 0.5 * (tracker + other_track) + new_grad - gradient
        gradient = new_grad
        weight = new_weight
    return (weight, tracker)


def solution(mesh):
    in_specs = (
        P(),
        P(None, "dp", None),
        P(None, "dp", None),
        P("dp", None),
        P("dp", None),
        P("dp", None),
        P(),
        P(),
        P("dp", None),
    )
    out_specs = (P("dp", None), P("dp", None))
    return jax.shard_map(shards, mesh=mesh, in_specs=in_specs, out_specs=out_specs, check_vma=False)
```

profile of v0, /device:TPU:2, one launch (start us, length us, event | category | flops | bytes accessed | tf_op | source)
XLA Modules:
  0.0 503.9 jit_solution(6264064592790391723)
XLA Ops:
  6.4 10.5 %all-to-all-start.1 = ((bf16[128,1,4]{2,1,0:T(2,128)(2,1)}), bf16[128,1,4]{2,1,0:T(2,128)(2,1)S(1)}, u32[]{:S(2)}, u32[]{:S(2)}) async-start(bf16[128,1,4]{2,1,0:T(2,128)(2,1)} %all_to_all.24), calls=%async_computation.1 | async-start | bytes 131072 | tf_op jit(solution)/shard_map/all_to_all | solution.py:81
  19.8 6.0 %all-to-all-done.1 = bf16[128,1,4]{2,1,0:T(2,128)(2,1)S(1)} async-done(((bf16[128,1,4]{2,1,0:T(2,128)(2,1)}), bf16[128,1,4]{2,1,0:T(2,128)(2,1)S(1)}, u32[]{:S(2)}, u32[]{:S(2)}) %all-to-all-start.1) | async-done | bytes 1056 | tf_op jit(solution)/shard_map/all_to_all | solution.py:81
  25.8 5.2 %all-to-all-start.3 = ((bf16[128,1,4]{2,1,0:T(2,128)(2,1)}), bf16[128,1,4]{2,1,0:T(2,128)(2,1)S(1)}, u32[]{:S(2)}, u32[]{:S(2)}) async-start(bf16[128,1,4]{2,1,0:T(2,128)(2,1)} %all_to_all.25), calls=%async_computation.3 | async-start | bytes 131072 | tf_op jit(solution)/shard_map/all_to_all | solution.py:81
  31.0 2.4 scatter_custom_fusion
  34.6 5.2 %all-to-all-done.3 = bf16[128,1,4]{2,1,0:T(2,128)(2,1)S(1)} async-done(((bf16[128,1,4]{2,1,0:T(2,128)(2,1)}), bf16[128,1,4]{2,1,0:T(2,128)(2,1)S(1)}, u32[]{:S(2)}, u32[]{:S(2)}) %all-to-all-start.3) | async-done | bytes 1056 | tf_op jit(solution)/shard_map/all_to_all | solution.py:81
  39.9 5.9 %all-to-all-start = ((bf16[128,4,1024]{2,1,0:T(4,128)(2,1)}), bf16[128,4,1024]{2,1,0:T(4,128)(2,1)}, u32[]{:S(2)}, u32[]{:S(2)}) async-start(bf16[128,4,1024]{2,1,0:T(4,128)(2,1)} %reshape.189), calls=%async_computation | async-start | bytes 2097152 | tf_op jit(solution)/shard_map/all_to_all | solution.py:80
  46.5 3.1 scatter_custom_fusion.2
  52.9 185.3 %conditional.2 = (f32[1024,1024]{1,0:T(8,128)}, f32[1024,1024]{1,0:T(8,128)}) conditional(s32[]{:T(128)} %clamp.6, (f32[1024,1024]{1,0:T(8,128)}, f32[1024,1024]{1,0:T(8,128)}) %tuple.64, (f32[1024,1024]{1,0:T(8,128)}, f32[1024,1024]{1,0:T(8,128)}) %tuple.64, (f32[1024,1024]{1,0:T(8,128)}, ...), branch_computations={%region_0.1_spmd, %region_1.2_spmd, %region_2.3_spmd, %region_3.4_... | conditional | bytes 33554528 | solution.py:85
  55.0 93.8 %collective-permute-done.2 = f32[1024,1024]{1,0:T(8,128)} collective-permute-done((f32[1024,1024]{1,0:T(8,128)}, f32[1024,1024]{1,0:T(8,128)}, u32[]{:S(2)}, u32[]{:S(2)}) %collective-permute-start.2) | collective-permute-done | bytes 4194336 | tf_op jit(solution)/shard_map/cond/branch_1_fun/ppermute | solution.py:15
  148.8 89.5 %collective-permute-done.3 = f32[1024,1024]{1,0:T(8,128)} collective-permute-done((f32[1024,1024]{1,0:T(8,128)}, f32[1024,1024]{1,0:T(8,128)}, u32[]{:S(2)}, u32[]{:S(2)}) %collective-permute-start.3) | collective-permute-done | bytes 4194336 | tf_op jit(solution)/shard_map/cond/branch_1_fun/ppermute | solution.py:15
  238.3 8.7 %multiply_subtract_fusion.1 = f32[1024,1024]{1,0:T(8,128)} fusion(f32[1024,1024]{1,0:T(8,128)} %param.27, f32[1024,1024]{1,0:T(8,128)} %param.26, f32[1024,1024]{1,0:T(8,128)} %get-tuple-element.90), kind=kLoop, calls=%fused_computation.9 | loop fusion | flops 4194304 | bytes 16777216 | tf_op jit(solution)/shard_map/sub | solution.py:88
  247.6 10.1 %all-to-all-start.2 = ((bf16[128,4,1024]{2,1,0:T(4,128)(2,1)}), bf16[128,4,1024]{2,1,0:T(4,128)(2,1)}, u32[]{:S(2)}, u32[]{:S(2)}) async-start(bf16[128,4,1024]{2,1,0:T(4,128)(2,1)} %reshape.197), calls=%async_computation.2 | async-start | bytes 2097152 | tf_op jit(solution)/shard_map/all_to_all | solution.py:80
  259.8 3.4 convolution_convert_fusion.3
  265.5 4.8 fusion.4
  272.6 3.0 multiply_convert_fusion.1
  278.1 6.1 %add_subtract_fusion.1 = (f32[1024,1024]{1,0:T(8,128)S(1)}, f32[1024,1024]{1,0:T(8,128)}) fusion(f32[1024,1024]{1,0:T(8,128)S(1)} %copy-done.11, f32[1024,1024]{1,0:T(8,128)S(1)} %copy-done.3, f32[1024,1024]{1,0:T(8,128)} %get-tuple-element.91, bf16[512,1024]{1,0:T(8,128)(2,1)S(1)} %copy-done.8, bf16[512,1024]{0,1:T(8,128)(2,1)S(1)} %bitcast.98), kind=kOutput, calls=%fused_computation.8 | convolution fusion | flops 1077936128 | bytes 23068672 | tf_op jit(solution)/shard_map/dot_general | solution.py:47
  286.2 184.1 %conditional.3 = (f32[1024,1024]{1,0:T(8,128)}, f32[1024,1024]{1,0:T(8,128)}) conditional(s32[]{:T(128)} %clamp.7, (f32[1024,1024]{1,0:T(8,128)S(1)}, f32[1024,1024]{1,0:T(8,128)S(1)}) %tuple.85, (f32[1024,1024]{1,0:T(8,128)S(1)}, f32[1024,1024]{1,0:T(8,128)S(1)}) %tuple.86, (f32[1024,1024]{1,0:T(8,128)S(1)}, ...), branch_computations={%region_12.13_spmd, %region_13.14_spmd, %region_14.15_spmd, %regio... | conditional | bytes 33554528 | solution.py:85
  286.2 3.0 collective-permute-start.18
  289.7 91.5 %collective-permute-done.18 = f32[1024,1024]{1,0:T(8,128)} collective-permute-done((f32[1024,1024]{1,0:T(8,128)S(1)}, f32[1024,1024]{1,0:T(8,128)}, u32[]{:S(2)}, u32[]{:S(2)}) %collective-permute-start.18) | collective-permute-done | bytes 4194336 | tf_op jit(solution)/shard_map/cond/branch_2_fun/ppermute | solution.py:15
  381.3 89.0 %collective-permute-done.19 = f32[1024,1024]{1,0:T(8,128)} collective-permute-done((f32[1024,1024]{1,0:T(8,128)S(1)}, f32[1024,1024]{1,0:T(8,128)}, u32[]{:S(2)}, u32[]{:S(2)}) %collective-permute-start.19) | collective-permute-done | bytes 4194336 | tf_op jit(solution)/shard_map/cond/branch_2_fun/ppermute | solution.py:15
  470.3 8.7 %multiply_subtract_fusion = f32[1024,1024]{1,0:T(8,128)} fusion(f32[1024,1024]{1,0:T(8,128)} %copy-done.1, f32[1024,1024]{1,0:T(8,128)} %multiply_subtract_fusion.1, f32[1024,1024]{1,0:T(8,128)} %get-tuple-element.92), kind=kLoop, calls=%fused_computation.7 | loop fusion | flops 4194304 | bytes 16777216 | tf_op jit(solution)/shard_map/sub | solution.py:88
  481.1 3.6 convolution_convert_fusion.2
  491.5 3.0 multiply_convert_fusion
  498.0 5.9 %add_subtract_fusion = f32[1024,1024]{1,0:T(8,128)} fusion(f32[1024,1024]{1,0:T(8,128)S(1)} %copy-done.5, f32[1024,1024]{1,0:T(8,128)S(1)} %copy-done.2, f32[1024,1024]{1,0:T(8,128)} %get-tuple-element.93, bf16[512,1024]{1,0:T(8,128)(2,1)S(1)} %copy-done.7, bf16[512,1024]{0,1:T(8,128)(2,1)S(1)} %bitcast.97), kind=kOutput, calls=%fused_computation.6 | convolution fusion | flops 1077936128 | bytes 18874368 | tf_op jit(solution)/shard_map/dot_general | solution.py:47
  (84 shorter events, 39.8 us)
Async XLA Ops:
  0.6 259.2 %copy-start = (bf16[1024,1024]{1,0:T(8,128)(2,1)S(1)}, bf16[1024,1024]{1,0:T(8,128)(2,1)}, u32[]{:S(2)}) copy-start(bf16[1024,1024]{1,0:T(8,128)(2,1)} %param.29) | copy-start | bytes 6291460
  2.5 47.1 %copy-start.14 = (bf16[128,1024]{1,0:T(8,128)(2,1)S(1)}, bf16[128,1024]{1,0:T(8,128)(2,1)}, u32[]{:S(2)}) copy-start(bf16[128,1024]{1,0:T(8,128)(2,1)} %param.30) | copy-start | bytes 786436
  6.4 19.4 %all-to-all-start.1 = ((bf16[128,1,4]{2,1,0:T(2,128)(2,1)}), bf16[128,1,4]{2,1,0:T(2,128)(2,1)S(1)}, u32[]{:S(2)}, u32[]{:S(2)}) async-start(bf16[128,1,4]{2,1,0:T(2,128)(2,1)} %all_to_all.24), calls=%async_computation.1 | async-start | bytes 131072 | tf_op jit(solution)/shard_map/all_to_all | solution.py:81
  25.8 14.1 %all-to-all-start.3 = ((bf16[128,1,4]{2,1,0:T(2,128)(2,1)}), bf16[128,1,4]{2,1,0:T(2,128)(2,1)S(1)}, u32[]{:S(2)}, u32[]{:S(2)}) async-start(bf16[128,1,4]{2,1,0:T(2,128)(2,1)} %all_to_all.25), calls=%async_computation.3 | async-start | bytes 131072 | tf_op jit(solution)/shard_map/all_to_all | solution.py:81
  34.6 15.9 %copy-start.13 = (f32[128,1024]{1,0:T(8,128)S(1)}, f32[128,1024]{1,0:T(8,128)}, u32[]{:S(2)}) copy-start(f32[128,1024]{1,0:T(8,128)} %param.31) | copy-start | bytes 1572868
  39.9 207.7 %all-to-all-start = ((bf16[128,4,1024]{2,1,0:T(4,128)(2,1)}), bf16[128,4,1024]{2,1,0:T(4,128)(2,1)}, u32[]{:S(2)}, u32[]{:S(2)}) async-start(bf16[128,4,1024]{2,1,0:T(4,128)(2,1)} %reshape.189), calls=%async_computation | async-start | bytes 2097152 | tf_op jit(solution)/shard_map/all_to_all | solution.py:80
  53.0 95.9 %collective-permute-start.2 = (f32[1024,1024]{1,0:T(8,128)}, f32[1024,1024]{1,0:T(8,128)}, u32[]{:S(2)}, u32[]{:S(2)}) collective-permute-start(f32[1024,1024]{1,0:T(8,128)} %get-tuple-element.58), channel_id=1, source_target_pairs={{0,2},{1,3},{2,0},{3,1},{4,6},{5,7},{6,4},{7,5},{8,10},{9,11},{10,... | collective-permute-start | bytes 12582920 | tf_op jit(solution)/shard_map/cond/branch_1_fun/ppermute | solution.py:15
  54.5 183.8 %collective-permute-start.3 = (f32[1024,1024]{1,0:T(8,128)}, f32[1024,1024]{1,0:T(8,128)}, u32[]{:S(2)}, u32[]{:S(2)}) collective-permute-start(f32[1024,1024]{1,0:T(8,128)} %get-tuple-element.59), channel_id=1, source_target_pairs={{0,2},{1,3},{2,0},{3,1},{4,6},{5,7},{6,4},{7,5},{8,10},{9,11},{10,... | collective-permute-start | bytes 12582920 | tf_op jit(solution)/shard_map/cond/branch_1_fun/ppermute | solution.py:15
  247.6 231.4 %all-to-all-start.2 = ((bf16[128,4,1024]{2,1,0:T(4,128)(2,1)}), bf16[128,4,1024]{2,1,0:T(4,128)(2,1)}, u32[]{:S(2)}, u32[]{:S(2)}) async-start(bf16[128,4,1024]{2,1,0:T(4,128)(2,1)} %reshape.197), calls=%async_computation.2 | async-start | bytes 2097152 | tf_op jit(solution)/shard_map/all_to_all | solution.py:80
  265.5 7.1 %copy-start.15 = (bf16[128,1024]{0,1:T(8,128)(2,1)S(1)}, bf16[128,1024]{0,1:T(8,128)(2,1)}, u32[]{:S(2)}) copy-start(bf16[128,1024]{0,1:T(8,128)(2,1)} %copy.38) | copy-start | bytes 786436
  272.6 3.0 copy-start.10
  272.6 4.5 copy-start.11
  275.6 2.2 copy-start.3
  275.6 2.5 copy-start.8
  278.1 6.1 %copy-start.4 = (f32[1024,1024]{1,0:T(8,128)S(1)}, f32[1024,1024]{1,0:T(8,128)}, u32[]{:S(2)}) copy-start(f32[1024,1024]{1,0:T(8,128)} %multiply_subtract_fusion.1) | copy-start | bytes 12582916
  284.2 2.0 copy-start.1
  286.2 95.1 %collective-permute-start.18 = (f32[1024,1024]{1,0:T(8,128)S(1)}, f32[1024,1024]{1,0:T(8,128)}, u32[]{:S(2)}, u32[]{:S(2)}) collective-permute-start(f32[1024,1024]{1,0:T(8,128)S(1)} %get-tuple-element.74), channel_id=1, source_target_pairs={{0,4},{1,5},{2,6},{3,7},{4,0},{5,1},{6,2},{7,3},{8,12},{9,13},{10,... | collective-permute-start | bytes 12582920 | tf_op jit(solution)/shard_map/cond/branch_2_fun/ppermute | solution.py:15
  289.2 181.1 %collective-permute-start.19 = (f32[1024,1024]{1,0:T(8,128)S(1)}, f32[1024,1024]{1,0:T(8,128)}, u32[]{:S(2)}, u32[]{:S(2)}) collective-permute-start(f32[1024,1024]{1,0:T(8,128)S(1)} %get-tuple-element.75), channel_id=1, source_target_pairs={{0,4},{1,5},{2,6},{3,7},{4,0},{5,1},{6,2},{7,3},{8,12},{9,13},{10,... | collective-permute-start | bytes 12582920 | tf_op jit(solution)/shard_map/cond/branch_2_fun/ppermute | solution.py:15
  481.1 3.6 copy-start.6
  481.1 3.6 copy-start.12
  491.5 3.0 copy-start.9
  491.5 4.5 copy-start.7
  494.5 2.2 copy-start.2
  494.6 3.5 copy-start.5
where the time goes:
time: 505 us; the launch traced here: 504 us
  waiting for transfers between devices  375 us (74%)
  starting transfers between devices  37.3 us (7%)
  local copies, waits for them, and re-layouts  35.7 us (7%)
  matrix products  34.7 us (7%)
  other arithmetic  19.5 us (4%)
    ppermute x4, waiting for transfers between devices, from_partner(): return lax.ppermute(value, axis, pairs)  364 us
    sub x2, other arithmetic, shards(): new_weight = 0.5 * (weight + other_weight) - 0.05 * tracker  17.4 us
    all_to_all x2, starting transfers between devices, shards(): lax.all_to_all(send_rows, 'dp', split_axis=0, concat_axis=0, tiled=True)  16 us
    all_to_all x2, starting transfers between devices, shards(): lax.all_to_all(send_flags, 'dp', split_axis=0, concat_axis=0, tiled=True)  15.7 us
    dot_general x2, matrix products, local_grad(): lax.dot_general(rows, dvalues, (((0,), (0,)), ((), ())), preferred_elemen...  11.9 us
    all_to_all x2, waiting for transfers between devices, shards(): lax.all_to_all(send_flags, 'dp', split_axis=0, concat_axis=0, tiled=True)  11.2 us
  transfers between devices with their start and end apart: 8, of which 6 were waited for; matrix products, arithmetic and copies ran while one was open for 11% of the time, Pallas kernels for 0%

commit v1 on v0

v1 whole, which is shorter than its diff:
```python
from functools import partial

import jax
import jax.numpy as jnp
from jax import lax
from jax.experimental import pallas as pl
from jax.experimental.pallas import tpu as pltpu
from jax.sharding import PartitionSpec as P

HEADS = 16
STEPS = 2
CAP = 4
CHUNKS = 8
MESH = pl.DeviceIdType.MESH
F32 = jnp.float32
BF16 = jnp.bfloat16


def axis_of(bit):
    return 0 if bit == 0 else 1 + (bit - 1) // 2


def tracking_kernel(
    b0, b1,
    x_hbm, y_hbm, g_hbm, r1_hbm, r2_hbm, kw_hbm, lat_hbm, tgt_hbm,
    ox_hbm, oy_hbm,
    x_v, y_v, g_v, xs, ys, xr, yr, x1s, x1r, y1s, y1r, w2,
    rows1, rows2, kw, lat, tgt, keys, att, att_t, att2, att2_t, acc, vals, dv,
    in_sem, small_sem, out_sem, xss, xrs, yss, yrs, x1ss, x1rs, y1ss, y1rs,
):
    me = lax.axis_index("dp")
    size = x_v.shape[0] // CHUNKS
    width = x_v.shape[1]
    pairs = width // 128
    shared = axis_of(b0) == axis_of(b1)

    def flip(where, bit):
        step = 2**bit
        return where + step * (1 - 2 * ((where // step) % 2))

    p1 = flip(me, b0)
    p2 = flip(me, b1)
    px = flip(p1, b1) if shared else p2
    peers = (p1, p2, px) if shared else (p1, p2)

    def part(ref, c):
        return ref.at[pl.ds(pl.multiple_of(c * size, size), size)]

    def send(src, dst, ss, rs, c, peer):
        return pltpu.make_async_remote_copy(
            src_ref=part(src, c), dst_ref=part(dst, c), send_sem=ss.at[c], recv_sem=rs.at[c],
            device_id=(peer,), device_id_type=MESH)

    def fetch(src, dst, k, c):
        return pltpu.make_async_copy(part(src, c), part(dst, c), in_sem.at[k, c])

    def put(src, dst, k, c):
        return pltpu.make_async_copy(part(src, c), part(dst, c), out_sem.at[k, c])

    def each(body):
        lax.fori_loop(0, CHUNKS, lambda c, carry: (body(c), carry)[1], 0)

    smalls = [pltpu.make_async_copy(a, b, small_sem.at[k]) for k, (a, b) in enumerate(
        ((r1_hbm, rows1), (kw_hbm, kw), (lat_hbm, lat), (r2_hbm, rows2), (tgt_hbm, tgt)))]

    each(lambda c: fetch(x_hbm, x_v, 0, c).start())
    each(lambda c: fetch(y_hbm, y_v, 1, c).start())
    for copy in smalls:
        copy.start()
    each(lambda c: fetch(g_hbm, g_v, 2, c).start())

    barrier = pltpu.get_barrier_semaphore()
    for peer in peers:
        pl.semaphore_signal(barrier, inc=1, device_id=(peer,), device_id_type=MESH)
    pl.semaphore_wait(barrier, len(peers))

    def first(c):
        fetch(x_hbm, x_v, 0, c).wait()
        part(xs, c)[...] = part(x_v, c)[...].astype(BF16)
        send(xs, xr, xss, xrs, c, p1).start()

    each(first)

    def second(c):
        fetch(y_hbm, y_v, 1, c).wait()
        part(ys, c)[...] = part(y_v, c)[...].astype(BF16)
        send(ys, yr, yss, yrs, c, p1).start()

    each(second)
    for copy in smalls:
        copy.wait()

    low = lax.broadcasted_iota(jnp.int32, (128, 128), 1) < 64
    zero = jnp.zeros((128, 128), BF16)

    def lanes(p, wide=128):
        return pl.ds(pl.multiple_of(p * wide, wide), wide)

    def stacked(block):
        return jnp.concatenate([jnp.where(low, block, zero), jnp.where(low, zero, block)], axis=0)

    def make_keys(rows):
        def body(p, carry):
            keys[:, lanes(p, 256)] = jnp.dot(
                rows[...], kw[:, lanes(p, 256)], preferred_element_type=F32).astype(BF16)
            return carry
        lax.fori_loop(0, width // 256, body, 0)

    def attend(p, a, a_t):
        query = stacked(lat[:, lanes(p)])
        key = keys[:, lanes(p)]
        over = (((1,), (1,)), ((), ()))
        score = lax.dot_general(query, key, over, preferred_element_type=F32)
        a[p] = jax.nn.sigmoid(score * 0.125 - 3.5).astype(BF16)
        score = lax.dot_general(key, query, over, preferred_element_type=F32)
        a_t[p] = jax.nn.sigmoid(score * 0.125 - 3.5).astype(BF16)

    def accumulate(rows, weight, c):
        acc[...] += jnp.dot(rows[:, lanes(c)], part(weight, c)[...], preferred_element_type=F32)

    def residuals(a, a_t):
        vals[...] = acc[...].astype(BF16)

        def body(p, carry):
            both = jnp.dot(a[p], vals[:, lanes(p)], preferred_element_type=F32)
            out = jnp.where(low, both[:128], both[128:])
            resid = ((out - tgt[:, lanes(p)]) * 0.0625).astype(BF16)
            dv[:, lanes(p)] = jnp.dot(a_t[p], stacked(resid), preferred_element_type=F32).astype(BF16)
            return carry
        lax.fori_loop(0, pairs, body, 0)

    def grad(rows, c):
        return lax.dot_general(
            rows[:, lanes(c)], dv[...], (((0,), (0,)), ((), ())), preferred_element_type=F32)

    make_keys(rows1)
    acc[...] = jnp.zeros_like(acc)

    def third(c):
        attend(c, att, att_t)
        send(xs, xr, xss, xrs, c, p1).wait_recv()
        x1 = 0.5 * (part(x_v, c)[...] + part(xr, c)[...].astype(F32)) - 0.05 * part(y_v, c)[...]
        part(x_v, c)[...] = x1
        part(x1s, c)[...] = x1.astype(BF16)
        accumulate(rows1, x1s, c)
        if not shared:
            send(x1s, x1r, x1ss, x1rs, c, px).start()

    each(third)
    residuals(att, att_t)
    make_keys(rows2)
    acc[...] = jnp.zeros_like(acc)

    def mix(c):
        send(x1s, x1r, x1ss, x1rs, c, px).wait_recv()
        x2 = 0.5 * (part(x_v, c)[...] + part(x1r, c)[...].astype(F32)) - 0.05 * part(y_v, c)[...]
        part(x_v, c)[...] = x2
        part(w2, c)[...] = x2.astype(BF16)
        accumulate(rows2, w2, c)
        put(x_v, ox_hbm, 0, c).start()

    def fourth(c):
        attend(c, att2, att2_t)
        fetch(g_hbm, g_v, 2, c).wait()
        g1 = grad(rows1, c)
        send(ys, yr, yss, yrs, c, p1).wait_recv()
        mine = part(y_v, c)[...]
        other = part(yr, c)[...].astype(F32)
        if shared:
            part(w2, c)[...] = (part(x_v, c)[...] + 0.05 * (mine - other)).astype(BF16)
        y1 = 0.5 * (mine + other) + g1 - part(g_v, c)[...]
        part(y_v, c)[...] = y1
        part(g_v, c)[...] = 0.5 * y1 - g1
        part(y1s, c)[...] = y1.astype(BF16)
        if shared:
            send(w2, x1r, x1ss, x1rs, c, px).start()
        send(y1s, y1r, y1ss, y1rs, c, p2).start()
        if not shared:
            mix(c)

    each(fourth)
    if shared:
        def later(c):
            send(w2, x1r, x1ss, x1rs, c, px).wait_send()
            mix(c)
        each(later)
    residuals(att2, att2_t)

    def last(c):
        g2 = grad(rows2, c)
        send(y1s, y1r, y1ss, y1rs, c, p2).wait_recv()
        part(g_v, c)[...] = part(g_v, c)[...] + 0.5 * part(y1r, c)[...].astype(F32) + g2
        put(g_v, oy_hbm, 1, c).start()

    each(last)

    def drain(c):
        send(xs, xr, xss, xrs, c, p1).wait_send()
        send(ys, yr, yss, yrs, c, p1).wait_send()
        send(y1s, y1r, y1ss, y1rs, c, p2).wait_send()
        if not shared:
            send(x1s, x1r, x1ss, x1rs, c, px).wait_send()
        put(x_v, ox_hbm, 0, c).wait()
        put(g_v, oy_hbm, 1, c).wait()

    each(drain)


def track(b0, b1, params, trackers, old_grads, rows1, rows2, key_weight, latents, targets):
    tall, width = params.shape
    win, count_lat = rows1.shape[0], latents.shape[0]
    pairs = width // 128
    half = pltpu.VMEM((tall, width), BF16)
    full = pltpu.VMEM((tall, width), F32)
    chunked = pltpu.SemaphoreType.DMA((CHUNKS,))
    hbm = pl.BlockSpec(memory_space=pl.ANY)
    return pl.pallas_call(
        partial(tracking_kernel, b0, b1),
        out_shape=(jax.ShapeDtypeStruct(params.shape, F32), jax.ShapeDtypeStruct(params.shape, F32)),
        in_specs=[hbm] * 8,
        out_specs=(hbm, hbm),
        scratch_shapes=[full] * 3 + [half] * 9 + [
            pltpu.VMEM((win, width), BF16), pltpu.VMEM((win, width), BF16),
            pltpu.VMEM((width, width), BF16), pltpu.VMEM((count_lat, width), BF16),
            pltpu.VMEM((count_lat, width), F32), pltpu.VMEM((win, width), BF16),
            pltpu.VMEM((pairs, 2 * count_lat, win), BF16), pltpu.VMEM((pairs, win, 2 * count_lat), BF16),
            pltpu.VMEM((pairs, 2 * count_lat, win), BF16), pltpu.VMEM((pairs, win, 2 * count_lat), BF16),
            pltpu.VMEM((win, width), F32), pltpu.VMEM((win, width), BF16), pltpu.VMEM((win, width), BF16),
            pltpu.SemaphoreType.DMA((3, CHUNKS)), pltpu.SemaphoreType.DMA((5,)), pltpu.SemaphoreType.DMA((2, CHUNKS)),
        ] + [chunked] * 8,
        name="tracking",
        compiler_params=pltpu.CompilerParams(
            collective_id=1 + b0, has_side_effects=True, vmem_limit_bytes=60 * 2**20),
    )(params, trackers, old_grads, rows1, rows2, key_weight, latents, targets)


def pack_rows(owner, token_rows, count_dev):
    rows = token_rows.shape[0]
    onehot = (owner[:, None] == jnp.arange(count_dev, dtype=jnp.int32)[None, :]).astype(BF16)
    order = jnp.arange(rows)
    before = (order[:, None] > order[None, :]).astype(BF16)
    counts = jnp.dot(before, onehot, preferred_element_type=F32)
    rank = jnp.sum(counts * onehot.astype(F32), axis=1).astype(jnp.int32)
    where = owner * CAP + rank
    slots = jnp.arange(count_dev * CAP, dtype=jnp.int32)
    place = (slots[:, None] == where[None, :]).astype(BF16)
    return jnp.dot(place, token_rows, preferred_element_type=F32).astype(BF16)


def shards(step_index, dest, tokens, params, trackers, old_grads, key_weight, latents, targets):
    count_dev = lax.axis_size("dp")
    logn = count_dev.bit_length() - 1
    width = tokens.shape[2]
    rows = []
    for step in range(STEPS):
        packed = pack_rows(dest[step, :, 0], tokens[step], count_dev).reshape(count_dev, CAP, width)
        rows.append(lax.all_to_all(packed, "dp", split_axis=0, concat_axis=0, tiled=True).reshape(-1, width))
    return lax.switch(
        step_index[0] % logn,
        [partial(track, bit, (bit + 1) % logn) for bit in range(logn)],
        params, trackers, old_grads, rows[0], rows[1], key_weight, latents, targets)


def solution(mesh):
    in_specs = (
        P(),
        P(None, "dp", None),
        P(None, "dp", None),
        P("dp", None),
        P("dp", None),
        P("dp", None),
        P(),
        P(),
        P("dp", None),
    )
    out_specs = (P("dp", None), P("dp", None))
    return jax.shard_map(shards, mesh=mesh, in_specs=in_specs, out_specs=out_specs, check_vma=False)
```

time: 505 us -> 173 us (0.34)
  waiting for transfers between devices: 375 us -> 31.6 us
  Pallas kernels: 0 us -> 104 us
  matrix products: 34.7 us -> 4.62 us
  local copies, waits for them, and re-layouts: 35.7 us -> 14.3 us
  starting transfers between devices: 37.3 us -> 16.5 us
  other arithmetic: 19.5 us -> 0.02 us
    ppermute x4 -> x0, waiting for transfers between devices: 364 us -> none  [from_partner(): return lax.ppermute(value, axis, pairs)]
    pallas_call x0 -> x1, Pallas kernels: none -> 104 us  [track(): pl.pallas_call(partial(tracking_kernel, b0, b1), out_shape=(jax.ShapeDtyp...]
    dot_general x12 -> x4, matrix products: 34.7 us -> 4.62 us  [the longest x2 3.95 us: pack_rows(): return jnp.dot(place, token_rows, preferred_element_type=F32).astype(BF16)]
    all_to_all x4 -> x2, waiting for transfers between devices: 11.2 us -> 31.6 us  [shards(): lax.all_to_all(packed, 'dp', split_axis=0, concat_axis=0, tiled=True)]
    sub x4 -> x0, other arithmetic: 17.4 us -> none  [the longest x2 17.4 us: shards(): new_weight = 0.5 * (weight + other_weight) - 0.05 * tracker]
    all_to_all x4 -> x2, starting transfers between devices: 31.7 us -> 16.5 us  [shards(): lax.all_to_all(packed, 'dp', split_axis=0, concat_axis=0, tiled=True)]
    scatter x4 -> x0, local copies, waits for them, and re-layouts: 9.88 us -> none  [the longest x2 5.56 us: pack_rows(): jnp.zeros((count_dev * cap, width), jnp.bfloat16).at[where].set(token_rows)]
    convert_element_type x6 -> x0, local copies, waits for them, and re-layouts: 9.31 us -> none  [the longest x2 4.55 us: local_grad(): jnp.dot(rows, weight.astype(jnp.bfloat16), preferred_element_type=jnp.flo...]
  transfers between devices with their start and end apart: 8 -> 2, of which waited for: 6 -> 2; matrix products, arithmetic and copies ran while one was open for 11% -> 3% of each run, Pallas kernels for 0% -> 0%
where the time goes in v1:
time: 173 us
  Pallas kernels  104 us (60%)
  waiting for transfers between devices  31.6 us (18%)
  starting transfers between devices  16.5 us (10%)
  local copies, waits for them, and re-layouts  14.3 us (8%)
  matrix products  4.62 us (3%)
    pallas_call x1, Pallas kernels, track(): pl.pallas_call(partial(tracking_kernel, b0, b1), out_shape=(jax.ShapeDtyp...  104 us
    all_to_all x2, waiting for transfers between devices, shards(): lax.all_to_all(packed, 'dp', split_axis=0, concat_axis=0, tiled=True)  31.6 us
    all_to_all x2, starting transfers between devices, shards(): lax.all_to_all(packed, 'dp', split_axis=0, concat_axis=0, tiled=True)  16.5 us
    unnamed x8, local copies, waits for them, and re-layouts  6.96 us
    dot_general x2, matrix products, pack_rows(): return jnp.dot(place, token_rows, preferred_element_type=F32).astype(BF16)  3.95 us
  transfers between devices with their start and end apart: 2, of which 2 were waited for; matrix products, arithmetic and copies ran while one was open for 3% of the time, Pallas kernels for 0%

profile of v1, /device:TPU:2, one launch (start us, length us, event | category | flops | bytes accessed | tf_op | source)
XLA Modules:
  0.0 172.9 jit_solution(8014371953434593722)
XLA Ops:
  0.6 0.7 fusion.12
  1.3 0.3 fusion.1
  1.7 1.5 convolution_convert_fusion
  3.2 1.2 reshape.40
  4.4 0.0 copy-start
  4.4 0.0 copy-start.1
  4.4 10.5 %all-to-all-start.1 = ((bf16[128,4,1024]{2,1,0:T(4,128)(2,1)}), bf16[128,4,1024]{2,1,0:T(4,128)(2,1)S(1)}, u32[]{:S(2)}, u32[]{:S(2)}) async-start(bf16[128,4,1024]{2,1,0:T(4,128)(2,1)} %reshape.40), calls=%async_computation.1 | async-start | bytes 2097152 | tf_op jit(solution)/shard_map/all_to_all | solution.py:257
  14.9 0.3 fusion
  15.3 2.5 %convolution_convert_fusion.1 = bf16[512,1024]{1,0:T(8,128)(2,1)} fusion(bf16[2,256,1024]{2,1,0:T(8,128)(2,1)} %param.18, s32[256]{0:T(256)S(1)} %convert_add_fusion.1), kind=kOutput, calls=%fused_computation.1 | convolution fusion | flops 269090816 | bytes 1573888 | tf_op jit(solution)/shard_map/dot_general | solution.py:247
  17.7 2.2 %reshape.38 = bf16[128,4,1024]{2,1,0:T(4,128)(2,1)} reshape(bf16[512,1024]{1,0:T(8,128)(2,1)} %convolution_convert_fusion.1) | data formatting | bytes 2097152 | tf_op jit(solution)/shard_map/reshape | solution.py:256
  20.0 13.7 %all-to-all-done.1 = bf16[128,4,1024]{2,1,0:T(4,128)(2,1)S(1)} async-done(((bf16[128,4,1024]{2,1,0:T(4,128)(2,1)}), bf16[128,4,1024]{2,1,0:T(4,128)(2,1)S(1)}, u32[]{:S(2)}, u32[]{:S(2)}) %all-to-all-start.1) | async-done | bytes 1048608 | tf_op jit(solution)/shard_map/all_to_all | solution.py:257
  33.7 5.9 %all-to-all-start = ((bf16[128,4,1024]{2,1,0:T(4,128)(2,1)}), bf16[128,4,1024]{2,1,0:T(4,128)(2,1)}, u32[]{:S(2)}, u32[]{:S(2)}) async-start(bf16[128,4,1024]{2,1,0:T(4,128)(2,1)} %reshape.38), calls=%async_computation | async-start | bytes 2097152 | tf_op jit(solution)/shard_map/all_to_all | solution.py:257
  40.3 17.9 %all-to-all-done = bf16[128,4,1024]{2,1,0:T(4,128)(2,1)} async-done(((bf16[128,4,1024]{2,1,0:T(4,128)(2,1)}), bf16[128,4,1024]{2,1,0:T(4,128)(2,1)}, u32[]{:S(2)}, u32[]{:S(2)}) %all-to-all-start) | async-done | bytes 1048608 | tf_op jit(solution)/shard_map/all_to_all | solution.py:257
  58.2 0.0 copy-done
  58.2 0.0 copy-done.1
  58.2 107.8 %conditional.1 = ((f32[1024,1024]{1,0:T(8,128)}, f32[1024,1024]{1,0:T(8,128)})) conditional(s32[]{:T(128)} %clamp.3, (f32[1024,1024]{1,0:T(8,128)}, f32[1024,1024]{1,0:T(8,128)}, f32[1024,1024]{1,0:T(8,128)}, bf16[128,4,1024]{2,1,0:T(4,128)(2,1)}, bf16[128,4,1024]{2,1,0:T(4,128)(2,1)S(1)}, ...), branch_computations={%region_2.3_spmd, %region_3.4_spmd, %region_4.5_spmd, %region_5.6_... | conditional | bytes 4194312 | solution.py:258
  58.2 2.1 %reshape.46.r1_hbm = bf16[512,1024]{1,0:T(8,128)(2,1)} reshape(bf16[128,4,1024]{2,1,0:T(4,128)(2,1)} %get-tuple-element.211) | data formatting | bytes 2097152 | tf_op jit(solution)/shard_map/reshape | solution.py:257
  60.3 1.1 reshape.53.r2_hbm
  61.4 104.3 %tracking.11 = (f32[1024,1024]{1,0:T(8,128)}, f32[1024,1024]{1,0:T(8,128)}) custom-call(f32[1024,1024]{1,0:T(8,128)} %get-tuple-element.246.x_hbm, f32[1024,1024]{1,0:T(8,128)} %get-tuple-element.253.y_hbm, f32[1024,1024]{1,0:T(8,128)} %get-tuple-element.260.g_hbm, bf16[512,1024]{1,0:T(8,128)(2,1)} %reshape.46.r1_hbm, bf16[512,1024]{1,0:T(8,128)(2,1)} %reshape.53.r2_hbm, ...), custom_call_target="tpu_custom_call" | custom-call | tf_op jit(solution)/shard_map/cond/branch_4_fun/tracking/pallas_call | solution.py:217
  166.0 0.0 copy-start.2
  166.0 4.9 %copy.84 = f32[1024,1024]{1,0:T(8,128)} copy(f32[1024,1024]{1,0:T(8,128)} %get-tuple-element.302) | data formatting | bytes 8388608
  170.9 0.0 copy-done.2
  170.9 2.0 %copy.85 = f32[1024,1024]{1,0:T(8,128)} copy(f32[1024,1024]{1,0:T(8,128)S(1)} %copy-done.2) | data formatting | bytes 8388608
  (2 shorter events, 0.0 us)
Async XLA Ops:
  4.4 53.8 %copy-start = (bf16[1024,1024]{1,0:T(8,128)(2,1)S(1)}, bf16[1024,1024]{1,0:T(8,128)(2,1)}, u32[]{:S(2)}) copy-start(bf16[1024,1024]{1,0:T(8,128)(2,1)} %param.22) | copy-start | bytes 6291460
  4.4 53.8 %copy-start.1 = (bf16[128,1024]{1,0:T(8,128)(2,1)S(1)}, bf16[128,1024]{1,0:T(8,128)(2,1)}, u32[]{:S(2)}) copy-start(bf16[128,1024]{1,0:T(8,128)(2,1)} %param.23) | copy-start | bytes 786436
  4.4 29.3 %all-to-all-start.1 = ((bf16[128,4,1024]{2,1,0:T(4,128)(2,1)}), bf16[128,4,1024]{2,1,0:T(4,128)(2,1)S(1)}, u32[]{:S(2)}, u32[]{:S(2)}) async-start(bf16[128,4,1024]{2,1,0:T(4,128)(2,1)} %reshape.40), calls=%async_computation.1 | async-start | bytes 2097152 | tf_op jit(solution)/shard_map/all_to_all | solution.py:257
  33.7 24.5 %all-to-all-start = ((bf16[128,4,1024]{2,1,0:T(4,128)(2,1)}), bf16[128,4,1024]{2,1,0:T(4,128)(2,1)}, u32[]{:S(2)}, u32[]{:S(2)}) async-start(bf16[128,4,1024]{2,1,0:T(4,128)(2,1)} %reshape.38), calls=%async_computation | async-start | bytes 2097152 | tf_op jit(solution)/shard_map/all_to_all | solution.py:257
  166.0 5.0 %copy-start.2 = (f32[1024,1024]{1,0:T(8,128)S(1)}, f32[1024,1024]{1,0:T(8,128)}, u32[]{:S(2)}) copy-start(f32[1024,1024]{1,0:T(8,128)} %get-tuple-element.303) | copy-start | bytes 12582916
